TPU v7x, 512 devices: a whole 4x8x8 slice. The times are simulated.
512 devices in a mesh: lon: 32 (over x, y), lat: 4 (over z_lo, core), lev: 4 (over z_hi).
Axes of the slice: x: 4, y: 8, z: 8 (z_hi: 4, z_lo: 2; z = z_hi * 2 + z_lo), core: 2. Of those that a mesh axis runs over, the one named last changes fastest.
Arguments:
- adjoint_field: float32 [12, 12, 128, 4096], P(None, 'lev', 'lat', 'lon'), may hold values from -6 to 6
- east_courant: float32 [12, 128, 4096], P('lev', 'lat', 'lon'), may hold values from -0.2 to 0.2
- north_courant: float32 [12, 128, 4096], P('lev', 'lat', 'lon'), may hold values from -0.2 to 0.2
- pole_courant: float32 [12, 4096], P('lev', 'lon'), may hold values from -0.2 to 0.2
- mix_fraction: float32 [12, 128, 4096], P('lev', 'lat', 'lon'), may hold values from 0.05 to 0.6
- detrain_share: float32 [12, 128, 4096], P('lev', 'lat', 'lon'), may hold values from 0.1 to 3
- sounding_owner: int32 [2, 32768, 1], P(None, ('lon', 'lat')), may hold values from 0 to 127; in each aligned block of 256 rows (0 to 255, 256 to 511, ..., all dimensions but the last counted through in order) at most 4 rows name the same one
- sounding_cell: int32 [2, 32768], P(None, ('lon', 'lat')), may hold values from 0 to 4095
- sounding_count: int32 [2, 128], P(None, ('lon', 'lat')), may hold values from 1 to 256, 20480 in all within a row
- sounding_forcing: float32 [2, 12, 32768], P(None, 'lev', ('lon', 'lat')), may hold values from -6 to 6
Outputs:
- earlier_adjoint: float32 [12, 12, 128, 4096], P(None, 'lev', 'lat', 'lon')
Inputs may be any that keep to these rules, and one draw needn't show every extreme that they name: `sounding_owner`: in each aligned block of 256 slots of one step (the slots of one device) no owner is named more than 4 times, a bound that some block reaches. `sounding_count`: each step's counts sum to 20480; at each step some device has exactly 256.
All inputs are finite; a program needn't handle non-finite values.
Results may differ from a plain program's by a relative error of at most 0.0001.
Values sent between devices are 32-bit elements; how exact they have to be, the bound alone decides.
A program may use at most 128 MiB of HBM per device.

v0:
```python
import jax
import jax.numpy as jnp
from jax import lax
from jax.sharding import PartitionSpec as P


def from_behind(value, axis, steps):
    count = lax.axis_size(axis)
    pairs = [(source, (source + steps) % count) for source in range(count)]
    return lax.ppermute(value, axis, pairs)


def from_behind_2(block, axis, distance):
    devices = range(lax.axis_size(axis))
    route = [(i - distance, i) for i in devices if i - distance in devices]
    return lax.ppermute(block, axis, route)


def extended(x, sides, width, wrap):
    for axis, dim in sides:
        size, length = (lax.axis_size(axis), x.shape[dim])
        up = [(i, (i + 1) % size) for i in range(size if wrap else size - 1)]
        down = [(j, i) for i, j in up]
        last = lax.slice_in_dim(x, length - width, length, axis=dim)
        initial = lax.slice_in_dim(x, 0, width, axis=dim)
        before = lax.ppermute(last, axis, up)
        after = lax.ppermute(initial, axis, down)
        x = jnp.concatenate([before, x, after], axis=dim)
    return x


def mix_sum(partial_sum):
    return lax.psum(partial_sum, "lev")


def on_device(
    adjoint_field,
    east_courant,
    north_courant,
    pole_courant,
    mix_fraction,
    detrain_share,
    sounding_owner,
    sounding_cell,
    sounding_count,
    sounding_forcing,
):
    lon_count = lax.axis_size("lon")
    lat_count = lax.axis_size("lat")
    lat_place = lax.axis_index("lat")
    owner_self = lax.axis_index("lon") * lat_count + lat_place
    tracers, lev_dev, lat_rows, lon_cols = adjoint_field.shape
    step_count = sounding_forcing.shape[0]
    slot_count = sounding_forcing.shape[2]
    grid_cells = lat_rows * lon_cols
    live_slots = jnp.arange(slot_count, dtype=jnp.int32)[None, :] < sounding_count
    values = jnp.where(live_slots[:, None, :], sounding_forcing, 0.0)
    owner_ids = sounding_owner[:, :, 0]
    step_ids = jnp.arange(step_count, dtype=jnp.int32)[:, None]
    index_pair = jnp.stack([owner_ids, sounding_cell], axis=1)
    all_values, all_pairs = (
        lax.all_gather(values, ("lon", "lat"), axis=2, tiled=True),
        lax.all_gather(index_pair, ("lon", "lat"), axis=2, tiled=True),
    )
    kept_values = jnp.where((all_pairs[:, 0, :] == owner_self)[:, None, :], all_values, 0.0)
    target_cells = all_pairs[:, 1, :]
    forcing_grid = (
        jnp.zeros((step_count, lev_dev, grid_cells), jnp.float32)
        .at[step_ids, :, target_cells]
        .add(jnp.swapaxes(kept_values, 1, 2))
    )
    forcing_grid = forcing_grid.reshape(step_count, lev_dev, lat_rows, lon_cols)
    west_column = from_behind(east_courant[:, :, -1:], "lon", 1)
    west_wind = jnp.concatenate([west_column, east_courant[:, :, :-1]], axis=2)
    south_row = from_behind_2(north_courant[:, -1:, :], "lat", 1)
    south_wind = jnp.concatenate([south_row, north_courant[:, :-1, :]], axis=1)
    pole_pair = jnp.stack([north_courant[:, -1, :], pole_courant], axis=0)
    partner_winds = from_behind(pole_pair, "lon", lon_count // 2)
    row_index = jnp.arange(lat_rows, dtype=jnp.int32)[None, :, None]
    at_top = jnp.logical_and(lat_place == lat_count - 1, row_index == lat_rows - 1)
    at_bottom = jnp.logical_and(lat_place == 0, row_index == 0)
    upwind_east = jnp.maximum(east_courant, 0.0)
    upwind_west = -jnp.minimum(west_wind, 0.0)
    upwind_north = jnp.maximum(north_courant, 0.0) + jnp.where(
        at_top, -jnp.minimum(partner_winds[0], 0.0)[:, None, :], 0.0
    )
    upwind_south = jnp.where(
        at_bottom,
        (jnp.maximum(pole_courant, 0.0) - jnp.minimum(partner_winds[1], 0.0))[:, None, :],
        -jnp.minimum(south_wind, 0.0),
    )
    total_detrain = lax.psum(jnp.sum(detrain_share, axis=0), "lev")
    adjoint = adjoint_field
    for position in range(step_count):
        step_now = step_count - 1 - position
        adjoint = adjoint + forcing_grid[step_now][None]
        partial_sum = jnp.sum(detrain_share[None] * adjoint, axis=1)
        column_sum = mix_sum(partial_sum)
        adjoint = (1.0 - mix_fraction)[None] * adjoint + mix_fraction[None] * (
            column_sum / total_detrain
        )[:, None]
        across = extended(adjoint, (("lon", 3),), 1, True)
        east_side = across[:, :, :, 2:]
        west_side = across[:, :, :, :-2]
        upright = extended(adjoint, (("lat", 2),), 1, False)
        north_side = upright[:, :, 2:, :]
        south_side = upright[:, :, :-2, :]
        edge_row = jnp.where(lat_place == 0, adjoint[:, :, :1, :], adjoint[:, :, -1:, :])
        partner_row = from_behind(edge_row, "lon", lon_count // 2)
        north_side = jnp.where(at_top, partner_row, north_side)
        south_side = jnp.where(at_bottom, partner_row, south_side)
        adjoint = (
            adjoint
            + upwind_east * (east_side - adjoint)
            + upwind_west * (west_side - adjoint)
            + upwind_north * (north_side - adjoint)
            + upwind_south * (south_side - adjoint)
        )
    return adjoint


def solution(mesh):
    return jax.shard_map(
        on_device,
        mesh=mesh,
        in_specs=(
            P(None, "lev", "lat", "lon"),
            P("lev", "lat", "lon"),
            P("lev", "lat", "lon"),
            P("lev", "lon"),
            P("lev", "lat", "lon"),
            P("lev", "lat", "lon"),
            P(None, ("lon", "lat"), None),
            P(None, ("lon", "lat")),
            P(None, ("lon", "lat")),
            P(None, "lev", ("lon", "lat")),
        ),
        out_specs=P(None, "lev", "lat", "lon"),
        check_vma=False,
    )
```

profile of v0, /device:TPU:1, one launch (start us, length us, event | category | flops | bytes accessed | tf_op | source)
XLA Modules:
  0.0 865.7 jit_solution(10978872272690706526)
XLA Ops:
  6.5 0.7 copy.54
  7.2 0.7 pad_add_fusion.1
  7.9 160.9 %all_gather.6 = s32[2,2,32768]{2,0,1:T(2,128)S(1)} all-gather(s32[2,2,256]{2,0,1:T(2,128)S(1)} %pad_add_fusion.1), channel_id=1, replica_groups=mesh['lon'=32,'lat'=4,'lev'=4] {'lon','lat'}, dimensions={2}, use_global_device_ids=true | all-gather | bytes 528384 | tf_op jit(solution)/shard_map/all_gather | solution.py:63
  168.9 0.1 compare_select_fusion
  169.0 0.1 broadcast_in_dim.137
  169.1 1.1 multiply_reduce_fusion.1
  170.3 1.4 and_reduce_fusion
  171.6 0.2 select_bitcast_fusion.1
  171.9 0.1 compare_bitcast_fusion
  172.0 0.1 iota_compare_fusion
  172.1 153.2 %all_gather.7 = f32[2,3,32768]{2,0,1:T(2,128)S(1)} all-gather(f32[2,3,256]{2,0,1:T(2,128)S(1)} %broadcast_select_fusion.2), channel_id=1, replica_groups=mesh['lon'=32,'lat'=4,'lev'=4] {'lon','lat'}, dimensions={2}, use_global_device_ids=true | all-gather | bytes 792576 | tf_op jit(solution)/shard_map/all_gather | solution.py:62
  325.3 0.5 select_bitcast_fusion
  325.8 16.6 %copy.38 = f32[2,32768,3]{2,1,0:T(8,128)} copy(f32[2,32768,3]{1,0,2:T(2,128)S(1)} %select_bitcast_fusion) | data formatting | bytes 1572864 | tf_op jit(solution)/shard_map/transpose | solution.py:70
  342.3 349.8 %scatter_custom_fusion = f32[3,8192]{0,1:T(8,128)} fusion(s32[65536]{0:T(1024)S(1)} %bitcast.41, f32[65536,3]{1,0:T(8,128)} %bitcast.36, f32[]{:T(128)} %constant.12.clone.1), kind=kCustom, calls=%fused_computation.1 | custom fusion | flops 196608 | bytes 98816
  692.1 3.9 fusion.43
  696.0 2.2 copy.24
  698.2 0.0 copy-done.1
  698.3 1.1 fusion.34
  699.4 0.0 all-reduce.3.cloned.1.call-update
  699.4 0.0 all-reduce.5.cloned.1.call-start
  699.5 3.4 collective-permute-start.6
  702.9 1.9 collective-permute-start.3
  704.8 0.1 slice.98
  704.9 1.9 collective-permute-start.1
  706.9 21.0 %psum.22 = f32[32,128]{1,0:T(8,128)S(1)} all-reduce(f32[32,128]{1,0:T(8,128)S(1)} %reduce_sum.28), channel_id=1, replica_groups=mesh['lon'=32,'lat'=4,'lev'=4] {'lev'}, use_global_device_ids=true, to_apply=%region_4.5 | all-reduce | flops 4096 | bytes 32768 | tf_op jit(solution)/shard_map/psum | solution.py:92
  727.9 0.6 copy.32
  728.5 0.1 fusion.35
  728.6 0.1 select_add_fusion
  728.7 21.9 %all-reduce.3.cloned.1.call-done = f32[12,32,128]{2,0,1:T(8,128)} async-done(((f32[12,32,128]{2,0,1:T(8,128)}), f32[12,32,128]{2,0,1:T(8,128)}) %all-reduce.3.cloned.1.call-update) | async-done | bytes 196624 | tf_op jit(solution)/shard_map/psum | solution.py:33
  750.6 1.0 broadcast_divide_fusion.1
  751.6 0.5 fusion.33
  752.1 0.3 fusion.45
  752.4 4.6 collective-permute-start.4
  757.0 4.9 collective-permute-start.5
  761.9 2.3 collective-permute-start.7
  764.2 0.3 copy.26
  764.5 5.2 collective-permute-start
  769.8 0.3 copy.28
  770.1 1.9 collective-permute-start.2
  772.0 0.1 fusion.37
  772.1 0.4 copy.27
  772.5 5.4 collective-permute-done.2
  777.9 0.4 copy.29
  778.4 0.6 copy-done.5
  779.0 0.0 copy-done.6
  779.0 0.6 copy-done.7
  779.6 2.3 multiply_reduce_fusion
  781.9 0.0 all-reduce.5.cloned.1.call-update
  781.9 47.8 %all-reduce.5.cloned.1.call-done = f32[12,32,128]{2,0,1:T(8,128)} async-done(((f32[12,32,128]{2,0,1:T(8,128)}), f32[12,32,128]{2,0,1:T(8,128)}) %all-reduce.5.cloned.1.call-update) | async-done | bytes 196624 | tf_op jit(solution)/shard_map/psum | solution.py:33
  829.8 1.0 broadcast_divide_fusion
  830.8 0.1 multiply_add_fusion
  830.9 4.6 collective-permute-start.10
  835.5 4.9 collective-permute-start.11
  840.5 2.3 collective-permute-start.12
  842.7 0.3 fusion.44
  843.0 0.3 copy.33
  843.4 5.1 collective-permute-start.8
  848.4 0.3 copy.35
  848.8 1.9 collective-permute-start.9
  850.7 0.4 copy.34
  851.1 5.5 collective-permute-done.9
  856.6 0.4 copy.36
  857.0 0.8 fusion.5
  857.8 1.0 copy.37
  (52 shorter events, 0.2 us)
Async XLA Ops:
  6.5 165.5 %copy-start.14 = (s32[2,1]{0,1:T(1,128)S(1)}, s32[2,1]{0,1:T(1,128)}, u32[]{:S(2)}) copy-start(s32[2,1]{0,1:T(1,128)} %param.18) | copy-start | bytes 28
  6.5 165.6 %copy-start.13 = (f32[2,3,256]{2,0,1:T(2,128)S(1)}, f32[2,3,256]{2,0,1:T(2,128)}, u32[]{:S(2)}) copy-start(f32[2,3,256]{2,0,1:T(2,128)} %param.19) | copy-start | bytes 18436
  6.5 744.1 %all-reduce.3.cloned.1.call-start = ((), (), s32[]{:S(2)}) async-start(), calls=%async_computation | async-start | bytes 524288 | tf_op jit(solution)/shard_map/psum | solution.py:33
  692.1 6.1 copy-start
  692.1 6.1 copy-start.1
  692.1 7.3 copy-start.4
  692.1 10.7 %copy-start.12 = (f32[3,128]{1,0:T(4,128)S(1)}, f32[3,128]{1,0:T(4,128)}, u32[]{:S(2)}) copy-start(f32[3,128]{1,0:T(4,128)} %param.13) | copy-start | bytes 4612
  692.1 12.7 %copy-start.2 = (f32[3,32,128]{2,1,0:T(8,128)S(1)}, f32[3,32,128]{2,1,0:T(8,128)}, u32[]{:S(2)}) copy-start(f32[3,32,128]{2,1,0:T(8,128)} %param.11) | copy-start | bytes 147460
  692.1 14.7 %copy-start.3 = (f32[3,32,128]{2,1,0:T(8,128)S(1)}, f32[3,32,128]{2,1,0:T(8,128)}, u32[]{:S(2)}) copy-start(f32[3,32,128]{2,1,0:T(8,128)} %param.14) | copy-start | bytes 147460
  699.4 130.4 %all-reduce.5.cloned.1.call-start = ((), (), s32[]{:S(2)}) async-start(), calls=%async_computation.1 | async-start | bytes 524288 | tf_op jit(solution)/shard_map/psum | solution.py:33
  699.5 29.1 %collective-permute-start.6 = (f32[3,1,128]{2,0,1:T(4,128)S(1)}, f32[3,1,128]{2,0,1:T(4,128)S(1)}, u32[]{:S(2)}, u32[]{:S(2)}) collective-permute-start(f32[3,1,128]{2,0,1:T(4,128)S(1)} %copy.55), channel_id=1, source_target_pairs={{0,4},{4,8},{8,12},{1,5},{5,9},{9,13},{2,6},{6,10},{10,14},{3,7},{... | collective-permute-start | bytes 4616 | tf_op jit(solution)/shard_map/ppermute | solution.py:16
  702.9 25.8 %collective-permute-start.3 = (f32[2,3,128]{2,1,0:T(4,128)S(1)}, f32[2,3,128]{2,1,0:T(4,128)S(1)}, u32[]{:S(2)}, u32[]{:S(2)}) collective-permute-start(f32[2,3,128]{2,1,0:T(4,128)S(1)} %pad_maximum_fusion.8), channel_id=1, source_target_pairs={{0,256},{16,272},{32,288},{48,304},{64,320},{80,336},{96,352},{112... | collective-permute-start | bytes 9224 | tf_op jit(solution)/shard_map/ppermute | solution.py:10
  704.9 23.6 %collective-permute-start.1 = (f32[3,32,1]{2,1,0:T(8,128)S(1)}, f32[3,32,1]{2,1,0:T(8,128)S(1)}, u32[]{:S(2)}, u32[]{:S(2)}) collective-permute-start(f32[3,32,1]{2,1,0:T(8,128)S(1)} %slice.98), channel_id=1, source_target_pairs={{0,16},{16,32},{32,48},{48,64},{64,80},{80,96},{96,112},{112,128},... | collective-permute-start | bytes 1160 | tf_op jit(solution)/shard_map/ppermute | solution.py:10
  706.9 57.7 %copy-start.10 = (pred[32]{0:T(512)(128)(4,1)}, pred[32]{0:T(512)(128)(4,1)S(1)}, u32[]{:S(2)}) copy-start(pred[32]{0:T(512)(128)(4,1)S(1)} %get-tuple-element.22) | copy-start | bytes 100
  706.9 65.1 %copy-start.8 = (pred[32]{0:T(512)(128)(4,1)}, pred[32]{0:T(512)(128)(4,1)S(1)}, u32[]{:S(2)}) copy-start(pred[32]{0:T(512)(128)(4,1)S(1)} %get-tuple-element.21) | copy-start | bytes 100
  752.4 26.0 %collective-permute-start.4 = (f32[12,3,1,128]{3,0,2,1:T(8,128)S(1)}, f32[12,3,1,128]{3,0,2,1:T(8,128)S(1)}, u32[]{:S(2)}, u32[]{:S(2)}) collective-permute-start(f32[12,3,1,128]{3,0,2,1:T(8,128)S(1)} %get-tuple-element.16), channel_id=1, source_target_pairs={{0,256},{16,272},{32,288},{48,304},{64,320},{80,336},{96,352},{112... | collective-permute-start | bytes 55304 | tf_op jit(solution)/shard_map/ppermute | solution.py:10
  757.0 21.4 %collective-permute-start.5 = (f32[12,3,1,128]{3,0,2,1:T(8,128)S(1)}, f32[12,3,1,128]{3,0,2,1:T(8,128)S(1)}, u32[]{:S(2)}, u32[]{:S(2)}) collective-permute-start(f32[12,3,1,128]{3,0,2,1:T(8,128)S(1)} %get-tuple-element.18), channel_id=1, source_target_pairs={{4,0},{8,4},{12,8},{5,1},{9,5},{13,9},{6,2},{10,6},{14,10},{7,3},{... | collective-permute-start | bytes 55304 | tf_op jit(solution)/shard_map/ppermute | solution.py:27
  761.9 16.5 %collective-permute-start.7 = (f32[12,3,1,128]{3,0,2,1:T(8,128)S(1)}, f32[12,3,1,128]{3,0,2,1:T(8,128)S(1)}, u32[]{:S(2)}, u32[]{:S(2)}) collective-permute-start(f32[12,3,1,128]{3,0,2,1:T(8,128)S(1)} %get-tuple-element.17), channel_id=1, source_target_pairs={{0,4},{4,8},{8,12},{1,5},{5,9},{9,13},{2,6},{6,10},{10,14},{3,7},{... | collective-permute-start | bytes 55304 | tf_op jit(solution)/shard_map/ppermute | solution.py:26
  764.5 7.6 collective-permute-start
  770.1 7.8 collective-permute-start.2
  778.4 0.6 copy-start.5
  778.4 0.6 copy-start.6
  779.0 0.6 copy-start.7
  830.8 26.3 %copy-start.9 = (pred[32]{0:T(512)(128)(4,1)S(1)}, pred[32]{0:T(512)(128)(4,1)}, u32[]{:S(2)}) copy-start(pred[32]{0:T(512)(128)(4,1)} %copy-done.8) | copy-start | bytes 100
  830.8 26.3 %copy-start.11 = (pred[32]{0:T(512)(128)(4,1)S(1)}, pred[32]{0:T(512)(128)(4,1)}, u32[]{:S(2)}) copy-start(pred[32]{0:T(512)(128)(4,1)} %copy-done.10) | copy-start | bytes 100
  830.9 26.1 %collective-permute-start.10 = (f32[12,3,1,128]{3,0,2,1:T(8,128)S(1)}, f32[12,3,1,128]{3,0,2,1:T(8,128)S(1)}, u32[]{:S(2)}, u32[]{:S(2)}) collective-permute-start(f32[12,3,1,128]{3,0,2,1:T(8,128)S(1)} %get-tuple-element.9), channel_id=1, source_target_pairs={{0,256},{16,272},{32,288},{48,304},{64,320},{80,336},{96,352},{112... | collective-permute-start | bytes 55304 | tf_op jit(solution)/shard_map/ppermute | solution.py:10
  835.5 21.5 %collective-permute-start.11 = (f32[12,3,1,128]{3,0,2,1:T(8,128)S(1)}, f32[12,3,1,128]{3,0,2,1:T(8,128)S(1)}, u32[]{:S(2)}, u32[]{:S(2)}) collective-permute-start(f32[12,3,1,128]{3,0,2,1:T(8,128)S(1)} %get-tuple-element.11), channel_id=1, source_target_pairs={{4,0},{8,4},{12,8},{5,1},{9,5},{13,9},{6,2},{10,6},{14,10},{7,3},{... | collective-permute-start | bytes 55304 | tf_op jit(solution)/shard_map/ppermute | solution.py:27
  840.5 16.6 %collective-permute-start.12 = (f32[12,3,1,128]{3,0,2,1:T(8,128)S(1)}, f32[12,3,1,128]{3,0,2,1:T(8,128)S(1)}, u32[]{:S(2)}, u32[]{:S(2)}) collective-permute-start(f32[12,3,1,128]{3,0,2,1:T(8,128)S(1)} %get-tuple-element.10), channel_id=1, source_target_pairs={{0,4},{4,8},{8,12},{1,5},{5,9},{9,13},{2,6},{6,10},{10,14},{3,7},{... | collective-permute-start | bytes 55304 | tf_op jit(solution)/shard_map/ppermute | solution.py:26
  843.4 7.3 collective-permute-start.8
  848.8 7.8 collective-permute-start.9
Sparse Core Ops, SparseCore 0:
  699.5 51.0 all-reduce.2
  782.1 47.6 all-reduce.4
where the time goes:
time: 866 us
  other arithmetic  361 us (42%)
  blocking collectives  335 us (39%)
  waiting for transfers between devices  80.7 us (9%)
  starting transfers between devices  44.9 us (5%)
  local copies, waits for them, and re-layouts  30 us (3%)
  between operations  13.9 us (2%)
    unnamed x4, other arithmetic  352 us
    all_gather x1, blocking collectives, on_device(): lax.all_gather(index_pair, ('lon', 'lat'), axis=2, tiled=True)  161 us
    all_gather x1, blocking collectives, on_device(): lax.all_gather(values, ('lon', 'lat'), axis=2, tiled=True)  153 us
    psum x2, waiting for transfers between devices, mix_sum(): return lax.psum(partial_sum, 'lev')  69.7 us
    psum x1, blocking collectives, on_device(): total_detrain = lax.psum(jnp.sum(detrain_share, axis=0), 'lev')  21 us
    ppermute x4, starting transfers between devices, extended(): after = lax.ppermute(initial, axis, down)  20.2 us
  transfers between devices with their start and end apart: 15, of which 4 were waited for; matrix products, arithmetic and copies ran while one was open for 0% of the time, Pallas kernels for 0%

commit v1 on v0

--- a/solution.py
+++ b/solution.py
@@ -60,7 +60,15 @@
     index_pair = jnp.stack([owner_ids, sounding_cell], axis=1)
     all_values, all_pairs = (
         lax.all_gather(values, ("lon", "lat"), axis=2, tiled=True),
-        lax.all_gather(index_pair, ("lon", "lat"), axis=2, tiled=True),
+        jnp.concatenate(
+            lax.all_to_all(
+                jnp.stack([index_pair] * lax.axis_size(("lon", "lat")), axis=0),
+                axis_name=("lon", "lat"),
+                split_axis=0,
+                concat_axis=0,
+            ),
+            axis=2,
+        ),
     )
     kept_values = jnp.where((all_pairs[:, 0, :] == owner_self)[:, None, :], all_values, 0.0)
     target_cells = all_pairs[:, 1, :]

time: 866 us -> 770 us (0.89)
  blocking collectives: 335 us -> 181 us
  waiting for transfers between devices: 80.7 us -> 103 us
  starting transfers between devices: 44.9 us -> 63.3 us
  other arithmetic: 361 us -> 372 us
    all_gather x1 -> x0, blocking collectives: 161 us -> none  [on_device(): lax.all_gather(index_pair, ('lon', 'lat'), axis=2, tiled=True)]
    psum x2, waiting for transfers between devices: 69.7 us -> 93.1 us  [mix_sum(): return lax.psum(partial_sum, 'lev')]
    all_to_all x0 -> x1, starting transfers between devices: none -> 14.2 us  [on_device(): lax.all_to_all(jnp.stack([index_pair] * lax.axis_size(('lon', 'lat')), ax...]
  transfers between devices with their start and end apart: 15 -> 16, of which waited for: 4 -> 4; matrix products, arithmetic and copies ran while one was open for 0% -> 2% of each run, Pallas kernels for 0% -> 0%
where the time goes in v1:
time: 770 us; the launch traced here: 768 us
  other arithmetic  372 us (48%)
  blocking collectives  181 us (24%)
  waiting for transfers between devices  103 us (13%)
  starting transfers between devices  63.3 us (8%)
  local copies, waits for them, and re-layouts  35.3 us (5%)
  between operations  13.9 us (2%)
    unnamed x4, other arithmetic  352 us
    all_gather x1, blocking collectives, on_device(): lax.all_gather(values, ('lon', 'lat'), axis=2, tiled=True)  161 us
    psum x2, waiting for transfers between devices, mix_sum(): return lax.psum(partial_sum, 'lev')  93.1 us
    psum x1, blocking collectives, on_device(): total_detrain = lax.psum(jnp.sum(detrain_share, axis=0), 'lev')  20.3 us
    ppermute x4, starting transfers between devices, extended(): after = lax.ppermute(initial, axis, down)  20 us
    ppermute x4, starting transfers between devices, from_behind(): return lax.ppermute(value, axis, pairs)  17.1 us
    transpose x1, local copies, waits for them, and re-layouts, on_device(): jnp.swapaxes(kept_values, 1, 2)  16.5 us
  transfers between devices with their start and end apart: 16, of which 4 were waited for; matrix products, arithmetic and copies ran while one was open for 2% of the time, Pallas kernels for 0%

profile of v1, /device:TPU:1, one launch (start us, length us, event | category | flops | bytes accessed | tf_op | source)
XLA Modules:
  0.0 768.2 jit_solution(7541160854112384592)
XLA Ops:
  6.5 0.7 copy.89
  7.2 0.7 pad_add_fusion.1
  7.9 0.9 stack.12
  8.9 14.2 %all-to-all-start = ((s32[128,2,2,256]{3,1,2,0:T(2,128)}), s32[128,2,2,256]{3,1,2,0:T(2,128)S(1)}, u32[]{:S(2)}, u32[]{:S(2)}) async-start(s32[128,2,2,256]{3,1,2,0:T(2,128)} %stack.12), calls=%async_computation | async-start | bytes 1048576 | tf_op jit(solution)/shard_map/all_to_all | solution.py:64
  23.1 0.7 slice.102
  23.9 3.5 collective-permute-start.6
  27.4 0.7 pad_maximum_fusion.8
  28.1 4.9 collective-permute-start.3
  33.0 0.9 slice.98
  33.9 3.1 collective-permute-start.1
  37.0 0.8 broadcast_maximum_fusion
  37.8 0.7 iota_compare_fusion
  38.5 0.8 reduce_sum.28
  39.3 20.3 %psum.22 = f32[32,128]{1,0:T(8,128)S(1)} all-reduce(f32[32,128]{1,0:T(8,128)S(1)} %reduce_sum.28), channel_id=1, replica_groups=mesh['lon'=32,'lat'=4,'lev'=4] {'lev'}, use_global_device_ids=true, to_apply=%region_4.5 | all-reduce | flops 4096 | bytes 32768 | tf_op jit(solution)/shard_map/psum | solution.py:100
  59.6 1.4 broadcast_subtract_fusion
  61.1 0.7 broadcast_select_fusion.2
  61.8 160.9 %all_gather.3 = f32[2,3,32768]{2,0,1:T(2,128)S(1)} all-gather(f32[2,3,256]{2,0,1:T(2,128)S(1)} %broadcast_select_fusion.2), channel_id=1, replica_groups=mesh['lon'=32,'lat'=4,'lev'=4] {'lon','lat'}, dimensions={2}, use_global_device_ids=true | all-gather | bytes 792576 | tf_op jit(solution)/shard_map/all_gather | solution.py:62
  222.7 1.5 fusion.35
  224.2 1.5 select_add_fusion
  225.8 0.3 reshape.134
  226.1 0.4 compare_select_fusion
  226.7 1.1 multiply_reduce_fusion.1
  227.8 1.3 and_reduce_fusion
  229.3 0.3 slice_compare_fusion
  229.6 0.2 copy.88
  229.8 0.5 select_bitcast_fusion
  230.3 16.5 %copy.70 = f32[2,32768,3]{2,1,0:T(8,128)} copy(f32[2,32768,3]{1,0,2:T(2,128)S(1)} %select_bitcast_fusion) | data formatting | bytes 1572864 | tf_op jit(solution)/shard_map/transpose | solution.py:78
  246.8 349.8 %scatter_custom_fusion = f32[3,8192]{0,1:T(8,128)} fusion(s32[65536]{0:T(1024)S(1)} %bitcast.47, f32[65536,3]{1,0:T(8,128)} %bitcast.40, f32[]{:T(128)} %constant.12.clone.1), kind=kCustom, calls=%fused_computation.1 | custom fusion | flops 196608 | bytes 98816
  596.5 3.9 fusion.43
  600.4 2.2 copy.56
  602.7 1.1 fusion.34
  603.9 45.2 %all-reduce.3.cloned.1.call-done = f32[12,32,128]{2,0,1:T(8,128)} async-done(((f32[12,32,128]{2,0,1:T(8,128)}), f32[12,32,128]{2,0,1:T(8,128)}) %all-reduce.3.cloned.1.call-update) | async-done | bytes 196624 | tf_op jit(solution)/shard_map/psum | solution.py:33
  649.1 1.0 broadcast_divide_fusion.1
  650.1 1.3 fusion.33
  651.4 1.4 fusion.45
  652.9 4.6 collective-permute-start.4
  657.4 4.9 collective-permute-start.5
  662.4 2.3 collective-permute-start.7
  664.7 1.4 copy.58
  666.1 5.0 collective-permute-start
  671.2 1.4 copy.60
  672.6 1.9 collective-permute-start.2
  674.5 0.9 fusion.37
  675.4 0.6 copy.64
  676.0 0.4 copy.59
  676.5 4.0 collective-permute-done.2
  680.4 0.4 copy.61
  680.9 2.4 multiply_reduce_fusion
  683.4 47.8 %all-reduce.5.cloned.1.call-done = f32[12,32,128]{2,0,1:T(8,128)} async-done(((f32[12,32,128]{2,0,1:T(8,128)}), f32[12,32,128]{2,0,1:T(8,128)}) %all-reduce.5.cloned.1.call-update) | async-done | bytes 196624 | tf_op jit(solution)/shard_map/psum | solution.py:33
  731.2 1.0 broadcast_divide_fusion
  732.2 1.3 multiply_add_fusion
  733.5 4.6 collective-permute-start.10
  738.1 4.9 collective-permute-start.11
  743.0 2.3 collective-permute-start.12
  745.3 0.3 fusion.44
  745.6 0.3 copy.65
  745.9 5.1 collective-permute-start.8
  751.0 0.3 copy.67
  751.3 1.9 collective-permute-start.9
  753.2 0.4 copy.66
  753.7 5.5 collective-permute-done.9
  759.1 0.4 copy.68
  759.6 0.8 fusion.5
  760.4 1.0 copy.69
  (49 shorter events, 0.7 us)
Async XLA Ops:
  6.5 220.1 %copy-start.10 = (s32[2]{0:T(128)S(1)}, s32[2]{0:T(128)}, u32[]{:S(2)}) copy-start(s32[2]{0:T(128)} %constant.41) | copy-start | bytes 28
  6.5 221.2 %copy-start.9 = (s32[2]{0:T(128)S(1)}, s32[2]{0:T(128)}, u32[]{:S(2)}) copy-start(s32[2]{0:T(128)} %constant.44) | copy-start | bytes 28
  8.9 216.8 %all-to-all-start = ((s32[128,2,2,256]{3,1,2,0:T(2,128)}), s32[128,2,2,256]{3,1,2,0:T(2,128)S(1)}, u32[]{:S(2)}, u32[]{:S(2)}) async-start(s32[128,2,2,256]{3,1,2,0:T(2,128)} %stack.12), calls=%async_computation | async-start | bytes 1048576 | tf_op jit(solution)/shard_map/all_to_all | solution.py:64
  23.1 626.0 %all-reduce.3.cloned.1.call-start = ((), (), s32[]{:S(2)}) async-start(), calls=%async_computation.1 | async-start | bytes 524288 | tf_op jit(solution)/shard_map/psum | solution.py:33
  23.9 200.3 %collective-permute-start.6 = (f32[3,1,128]{2,0,1:T(4,128)S(1)}, f32[3,1,128]{2,0,1:T(4,128)S(1)}, u32[]{:S(2)}, u32[]{:S(2)}) collective-permute-start(f32[3,1,128]{2,0,1:T(4,128)S(1)} %copy.90), channel_id=1, source_target_pairs={{0,4},{4,8},{8,12},{1,5},{5,9},{9,13},{2,6},{6,10},{10,14},{3,7},{... | collective-permute-start | bytes 4616 | tf_op jit(solution)/shard_map/ppermute | solution.py:16
  28.1 196.1 %collective-permute-start.3 = (f32[2,3,128]{2,1,0:T(4,128)S(1)}, f32[2,3,128]{2,1,0:T(4,128)S(1)}, u32[]{:S(2)}, u32[]{:S(2)}) collective-permute-start(f32[2,3,128]{2,1,0:T(4,128)S(1)} %pad_maximum_fusion.8), channel_id=1, source_target_pairs={{0,256},{16,272},{32,288},{48,304},{64,320},{80,336},{96,352},{112... | collective-permute-start | bytes 9224 | tf_op jit(solution)/shard_map/ppermute | solution.py:10
  33.9 188.8 %collective-permute-start.1 = (f32[3,32,1]{2,1,0:T(8,128)S(1)}, f32[3,32,1]{2,1,0:T(8,128)S(1)}, u32[]{:S(2)}, u32[]{:S(2)}) collective-permute-start(f32[3,32,1]{2,1,0:T(8,128)S(1)} %slice.98), channel_id=1, source_target_pairs={{0,16},{16,32},{32,48},{48,64},{64,80},{80,96},{96,112},{112,128},... | collective-permute-start | bytes 1160 | tf_op jit(solution)/shard_map/ppermute | solution.py:10
  596.5 6.1 copy-start
  596.5 6.1 copy-start.2
  596.5 7.3 copy-start.8
  602.7 46.4 %copy-start.5 = (f32[3,32,128]{2,1,0:T(8,128)}, f32[3,32,128]{2,1,0:T(8,128)S(1)}, u32[]{:S(2)}) copy-start(f32[3,32,128]{2,1,0:T(8,128)S(1)} %copy.56) | copy-start | bytes 147460
  603.8 127.4 %all-reduce.5.cloned.1.call-start = ((), (), s32[]{:S(2)}) async-start(), calls=%async_computation.2 | async-start | bytes 524288 | tf_op jit(solution)/shard_map/psum | solution.py:33
  651.4 29.5 %copy-start.1 = (f32[3,32,128]{2,1,0:T(8,128)S(1)}, f32[3,32,128]{2,1,0:T(8,128)}, u32[]{:S(2)}) copy-start(f32[3,32,128]{2,1,0:T(8,128)} %select_add_fusion) | copy-start | bytes 147460
  651.4 29.5 %copy-start.3 = (f32[3,32,128]{2,1,0:T(8,128)S(1)}, f32[3,32,128]{2,1,0:T(8,128)}, u32[]{:S(2)}) copy-start(f32[3,32,128]{2,1,0:T(8,128)} %param.15) | copy-start | bytes 147460
  651.4 29.5 %copy-start.4 = (f32[3,32,128]{2,1,0:T(8,128)S(1)}, f32[3,32,128]{2,1,0:T(8,128)}, u32[]{:S(2)}) copy-start(f32[3,32,128]{2,1,0:T(8,128)} %fusion.35) | copy-start | bytes 147460
  652.9 28.0 %collective-permute-start.4 = (f32[12,3,1,128]{3,0,2,1:T(8,128)S(1)}, f32[12,3,1,128]{3,0,2,1:T(8,128)S(1)}, u32[]{:S(2)}, u32[]{:S(2)}) collective-permute-start(f32[12,3,1,128]{3,0,2,1:T(8,128)S(1)} %get-tuple-element.16), channel_id=1, source_target_pairs={{0,256},{16,272},{32,288},{48,304},{64,320},{80,336},{96,352},{112... | collective-permute-start | bytes 55304 | tf_op jit(solution)/shard_map/ppermute | solution.py:10
  657.4 23.4 %collective-permute-start.5 = (f32[12,3,1,128]{3,0,2,1:T(8,128)S(1)}, f32[12,3,1,128]{3,0,2,1:T(8,128)S(1)}, u32[]{:S(2)}, u32[]{:S(2)}) collective-permute-start(f32[12,3,1,128]{3,0,2,1:T(8,128)S(1)} %get-tuple-element.18), channel_id=1, source_target_pairs={{4,0},{8,4},{12,8},{5,1},{9,5},{13,9},{6,2},{10,6},{14,10},{7,3},{... | collective-permute-start | bytes 55304 | tf_op jit(solution)/shard_map/ppermute | solution.py:27
  662.4 18.5 %collective-permute-start.7 = (f32[12,3,1,128]{3,0,2,1:T(8,128)S(1)}, f32[12,3,1,128]{3,0,2,1:T(8,128)S(1)}, u32[]{:S(2)}, u32[]{:S(2)}) collective-permute-start(f32[12,3,1,128]{3,0,2,1:T(8,128)S(1)} %get-tuple-element.17), channel_id=1, source_target_pairs={{0,4},{4,8},{8,12},{1,5},{5,9},{9,13},{2,6},{6,10},{10,14},{3,7},{... | collective-permute-start | bytes 55304 | tf_op jit(solution)/shard_map/ppermute | solution.py:26
  666.1 9.9 %collective-permute-start = (f32[12,3,32,1]{2,3,1,0:T(1,128)S(1)}, f32[12,3,32,1]{2,3,1,0:T(1,128)S(1)}, u32[]{:S(2)}, u32[]{:S(2)}) collective-permute-start(f32[12,3,32,1]{2,3,1,0:T(1,128)S(1)} %copy.58), channel_id=1, source_target_pairs={{16,0},{32,16},{48,32},{64,48},{80,64},{96,80},{112,96},{128,112},... | collective-permute-start | bytes 13832 | tf_op jit(solution)/shard_map/ppermute | solution.py:27
  672.6 7.8 %collective-permute-start.2 = (f32[12,3,32,1]{2,3,1,0:T(1,128)S(1)}, f32[12,3,32,1]{2,3,1,0:T(1,128)S(1)}, u32[]{:S(2)}, u32[]{:S(2)}) collective-permute-start(f32[12,3,32,1]{2,3,1,0:T(1,128)S(1)} %copy.60), channel_id=1, source_target_pairs={{0,16},{16,32},{32,48},{48,64},{64,80},{80,96},{96,112},{112,128},... | collective-permute-start | bytes 13832 | tf_op jit(solution)/shard_map/ppermute | solution.py:26
  675.4 56.8 %copy-start.6 = (f32[3,32,128]{2,1,0:T(8,128)S(1)}, f32[3,32,128]{2,1,0:T(8,128)}, u32[]{:S(2)}) copy-start(f32[3,32,128]{2,1,0:T(8,128)} %param.14) | copy-start | bytes 147460
  675.4 56.8 %copy-start.7 = (f32[3,32,128]{2,1,0:T(8,128)S(1)}, f32[3,32,128]{2,1,0:T(8,128)}, u32[]{:S(2)}) copy-start(f32[3,32,128]{2,1,0:T(8,128)} %broadcast_subtract_fusion) | copy-start | bytes 147460
  733.5 26.1 %collective-permute-start.10 = (f32[12,3,1,128]{3,0,2,1:T(8,128)S(1)}, f32[12,3,1,128]{3,0,2,1:T(8,128)S(1)}, u32[]{:S(2)}, u32[]{:S(2)}) collective-permute-start(f32[12,3,1,128]{3,0,2,1:T(8,128)S(1)} %get-tuple-element.9), channel_id=1, source_target_pairs={{0,256},{16,272},{32,288},{48,304},{64,320},{80,336},{96,352},{112... | collective-permute-start | bytes 55304 | tf_op jit(solution)/shard_map/ppermute | solution.py:10
  738.1 21.5 %collective-permute-start.11 = (f32[12,3,1,128]{3,0,2,1:T(8,128)S(1)}, f32[12,3,1,128]{3,0,2,1:T(8,128)S(1)}, u32[]{:S(2)}, u32[]{:S(2)}) collective-permute-start(f32[12,3,1,128]{3,0,2,1:T(8,128)S(1)} %get-tuple-element.11), channel_id=1, source_target_pairs={{4,0},{8,4},{12,8},{5,1},{9,5},{13,9},{6,2},{10,6},{14,10},{7,3},{... | collective-permute-start | bytes 55304 | tf_op jit(solution)/shard_map/ppermute | solution.py:27
  743.0 16.6 %collective-permute-start.12 = (f32[12,3,1,128]{3,0,2,1:T(8,128)S(1)}, f32[12,3,1,128]{3,0,2,1:T(8,128)S(1)}, u32[]{:S(2)}, u32[]{:S(2)}) collective-permute-start(f32[12,3,1,128]{3,0,2,1:T(8,128)S(1)} %get-tuple-element.10), channel_id=1, source_target_pairs={{0,4},{4,8},{8,12},{1,5},{5,9},{9,13},{2,6},{6,10},{10,14},{3,7},{... | collective-permute-start | bytes 55304 | tf_op jit(solution)/shard_map/ppermute | solution.py:26
  745.9 7.3 collective-permute-start.8
  751.3 7.8 %collective-permute-start.9 = (f32[12,3,32,1]{2,3,1,0:T(1,128)S(1)}, f32[12,3,32,1]{2,3,1,0:T(1,128)S(1)}, u32[]{:S(2)}, u32[]{:S(2)}) collective-permute-start(f32[12,3,32,1]{2,3,1,0:T(1,128)S(1)} %copy.67), channel_id=1, source_target_pairs={{0,16},{16,32},{32,48},{48,64},{64,80},{80,96},{96,112},{112,128},... | collective-permute-start | bytes 13832 | tf_op jit(solution)/shard_map/ppermute | solution.py:26
Sparse Core Ops, SparseCore 0:
  603.9 45.1 all-reduce.2
  683.5 47.6 all-reduce.4
